TPU v7x, 512 devices: a whole 4x4x16 slice. The times are simulated.
512 devices in a mesh: seq: 64 (over z, y), tp: 8 (over x, core).
Axes of the slice: x: 4, y: 4, z: 16, core: 2. Of those that a mesh axis runs over, the one named last changes fastest.
Arguments:
- query_proj: bfloat16 [4096, 8192], P('tp', 'seq'), may hold values from -6 to 6
- key_proj: bfloat16 [4096, 8192], P('tp', 'seq'), may hold values from -6 to 6
- value_proj: bfloat16 [4096, 8192], P('tp', 'seq'), may hold values from -6 to 6
- short_taps: float32 [3, 3, 4096], P(None, None, 'tp'), may hold values from -3.5 to 3.5
- long_filters: float32 [4096, 8192], P(('tp', 'seq')), may hold values from -2 to 2
- out_weight: bfloat16 [4096, 8192], P('seq', 'tp'), may hold values from -0.09375 to 0.09375
Outputs:
- block_out: bfloat16 [8192, 8192], P('seq', 'tp')
All inputs are finite; a program needn't handle non-finite values.
Results may differ from a plain program's by a relative error of at most 0.0058.
Values may be sent and summed in bfloat16 or wider, within the bound.
A program may use at most 64 MiB of HBM per device.

v0:
```python
import math
import jax
import jax.numpy as jnp
from jax import lax
from jax.sharding import PartitionSpec as P

precise = lax.Precision.HIGHEST


def shifted(value, axis, steps):
    count = lax.axis_size(axis)
    initial, last = (max(0, -steps), min(count, count - steps))
    return lax.ppermute(value, axis, [(source, source + steps) for source in range(initial, last)])


def short_filter(extended, tap_weights):
    return (
        tap_weights[0][:, None] * extended[:, 2:]
        + tap_weights[1][:, None] * extended[:, 1:-1]
        + tap_weights[2][:, None] * extended[:, :-2]
    )


def phase_table(period, out_size, in_size, direction):
    out_index = lax.broadcasted_iota(jnp.int32, (out_size, in_size), 0)
    in_index = lax.broadcasted_iota(jnp.int32, (out_size, in_size), 1)
    phase_angle = (out_index * in_index % period).astype(jnp.float32) * (
        direction * 2.0 * math.pi / period
    )
    return (jnp.cos(phase_angle), jnp.sin(phase_angle))


def left_apply(phase, signal):
    return jnp.einsum("kn,cnm->ckm", phase, signal, precision=precise)


def right_apply(signal, phase):
    return jnp.einsum("ckn,nm->ckm", signal, phase, precision=precise)


def forward_spectrum(signal, inner_size):
    channels_here, length = signal.shape
    period = 2 * length
    outer_size = period // inner_size
    blocks = signal.reshape(channels_here, outer_size // 2, inner_size)
    left_re, left_im = phase_table(outer_size, outer_size, outer_size // 2, -1.0)
    section_re = left_apply(left_re, blocks)
    section_im = left_apply(left_im, blocks)
    twist_re, twist_im = phase_table(period, outer_size, inner_size, -1.0)
    turned_re = section_re * twist_re - section_im * twist_im
    turned_im = section_re * twist_im + section_im * twist_re
    right_re, right_im = phase_table(inner_size, inner_size, inner_size, -1.0)
    spec_re = right_apply(turned_re, right_re) - right_apply(turned_im, right_im)
    spec_im = right_apply(turned_re, right_im) + right_apply(turned_im, right_re)
    return (spec_re, spec_im)


def inverse_signal(spec_re, spec_im, length, inner_size):
    channels_here = spec_re.shape[0]
    period = 2 * length
    outer_size = period // inner_size
    right_re, right_im = phase_table(inner_size, inner_size, inner_size, 1.0)
    mid_re = right_apply(spec_re, right_re) - right_apply(spec_im, right_im)
    mid_im = right_apply(spec_re, right_im) + right_apply(spec_im, right_re)
    twist_re, twist_im = phase_table(period, outer_size, inner_size, 1.0)
    turned_re = mid_re * twist_re - mid_im * twist_im
    turned_im = mid_re * twist_im + mid_im * twist_re
    left_re, left_im = phase_table(outer_size, outer_size // 2, outer_size, 1.0)
    signal = left_apply(left_re, turned_re) - left_apply(left_im, turned_im)
    return signal.reshape(channels_here, length) / period


def long_convolve(signal, filters, inner_size):
    length = signal.shape[1]
    data_re, data_im = forward_spectrum(signal, inner_size)
    filt_re, filt_im = forward_spectrum(filters, inner_size)
    prod_re = data_re * filt_re - data_im * filt_im
    prod_im = data_re * filt_im + data_im * filt_re
    return inverse_signal(prod_re, prod_im, length, inner_size)


def shards(query_proj, key_proj, value_proj, short_taps, long_filters, out_weight):
    tok_rows = query_proj.shape[1]
    inner_size = tok_rows // 2
    tail_cols = jnp.stack([query_proj[:, -2:], key_proj[:, -2:], value_proj[:, -2:]])
    before = shifted(tail_cols, "seq", 1)
    shorts = []
    for stream_index, stream in enumerate((query_proj, key_proj, value_proj)):
        extended = jnp.concatenate([before[stream_index], stream], axis=1).astype(jnp.float32)
        shorts.append(short_filter(extended, short_taps[stream_index]))
    query_short, key_short, value_short = shorts
    product = (key_short * value_short).astype(jnp.bfloat16)
    spread = lax.all_to_all(product, "seq", split_axis=0, concat_axis=1, tiled=True)
    mixed_conv = long_convolve(spread.astype(jnp.float32), long_filters, inner_size)
    returned = lax.all_to_all(mixed_conv, "seq", split_axis=1, concat_axis=0, tiled=True)
    gated_out = (query_short * returned).astype(jnp.bfloat16)
    full_rows = lax.all_gather(gated_out, "tp", axis=0, tiled=True)
    result = lax.dot_general(
        full_rows,
        lax.all_gather(out_weight, "seq", axis=0, tiled=True),
        (((0,), (0,)), ((), ())),
        preferred_element_type=jnp.float32,
    )
    return result.astype(jnp.bfloat16)


def solution(mesh):
    return jax.shard_map(
        shards,
        mesh=mesh,
        in_specs=(
            P("tp", "seq"),
            P("tp", "seq"),
            P("tp", "seq"),
            P(None, None, "tp"),
            P(("tp", "seq"), None),
            P("seq", "tp"),
        ),
        out_specs=P("seq", "tp"),
        check_vma=False,
    )
```

profile of v0, /device:TPU:2, one launch (start us, length us, event | category | flops | bytes accessed | tf_op | source)
XLA Modules:
  0.0 292.9 jit_solution(1270531788461723805)
XLA Ops:
  6.5 0.0 copy-start.1
  6.5 0.0 copy-start
  6.5 1.0 slice.94
  7.6 0.1 copy.35
  7.7 1.0 slice.95
  8.7 0.1 copy.36
  8.8 1.0 slice.96
  9.9 0.1 copy.37
  10.0 0.3 copy.25
  10.3 3.5 %collective-permute-start = (bf16[3,512,2]{2,1,0:T(8,128)(2,1)S(1)}, bf16[3,512,2]{2,1,0:T(8,128)(2,1)S(1)}, u32[]{:S(2)}, u32[]{:S(2)}) collective-permute-start(bf16[3,512,2]{2,1,0:T(8,128)(2,1)S(1)} %copy.25), channel_id=1, source_target_pairs={{0,8},{8,16},{16,24},{24,32},{32,40},{40,48},{48,56},{56,64},{64,7... | collective-permute-start | bytes 18440 | tf_op jit(solution)/shard_map/ppermute | solution.py:13
  13.8 0.3 multiply_sine_fusion.1
  14.1 1.1 reshape.82
  15.2 0.2 copy.29
  15.4 1.1 fusion.58
  16.5 1.1 fusion.61
  17.6 0.9 fusion.180
  18.4 0.8 fusion.4
  19.2 0.8 convolution_add_fusion.1
  20.0 0.3 multiply_sine_fusion
  20.3 1.8 collective-permute-done
  22.1 0.0 copy-done.1
  22.1 0.0 copy-done
  22.2 0.2 maximum_convert_fusion.1
  22.4 1.4 fusion.47
  23.8 20.5 %all-to-all-start = ((bf16[64,8,128]{2,1,0:T(8,128)(2,1)}), bf16[64,8,128]{2,1,0:T(8,128)(2,1)S(1)}, u32[]{:S(2)}, u32[]{:S(2)}) async-start(bf16[64,8,128]{2,1,0:T(8,128)(2,1)} %fusion.47), calls=%async_computation | async-start | bytes 262144 | tf_op jit(solution)/shard_map/all_to_all | solution.py:93
  44.3 0.8 fusion.6
  45.1 0.8 convolution_subtract_fusion.1
  45.9 15.1 %all-to-all-done = bf16[64,8,128]{2,1,0:T(8,128)(2,1)S(1)} async-done(((bf16[64,8,128]{2,1,0:T(8,128)(2,1)}), bf16[64,8,128]{2,1,0:T(8,128)(2,1)S(1)}, u32[]{:S(2)}, u32[]{:S(2)}) %all-to-all-start) | async-done | bytes 131104 | tf_op jit(solution)/shard_map/all_to_all | solution.py:93
  61.0 0.1 reshape.81
  61.1 0.9 convolution_bitcast_fusion
  62.0 0.9 convolution_bitcast_fusion.1
  62.9 0.8 fusion.48
  63.7 0.8 fusion.49
  64.5 0.0 copy-start.2
  64.5 0.8 convolution_subtract_fusion.2
  65.3 0.9 multiply_add_fusion
  66.2 0.7 fusion.71
  67.0 0.7 fusion.67
  67.7 0.7 convolution_subtract_fusion
  68.5 0.7 convolution_add_fusion
  69.2 1.1 fusion.11
  70.3 1.1 fusion.1
  71.4 0.2 copy.31
  71.6 0.1 div.13
  71.7 1.1 copy.32
  72.8 4.6 %all-to-all-start.1 = ((f32[8,64,128]{2,0,1:T(8,128)}), f32[8,64,128]{2,0,1:T(8,128)S(1)}, u32[]{:S(2)}, u32[]{:S(2)}) async-start(f32[8,64,128]{2,0,1:T(8,128)} %copy.32), calls=%async_computation.1 | async-start | bytes 524288 | tf_op jit(solution)/shard_map/all_to_all | solution.py:95
  77.4 0.0 all-gather.3.cloned.1.call-start
  77.5 0.0 copy-done.2
  77.5 0.1 maximum_convert_fusion
  77.6 21.1 %all-to-all-done.1 = f32[8,64,128]{2,0,1:T(8,128)S(1)} async-done(((f32[8,64,128]{2,0,1:T(8,128)}), f32[8,64,128]{2,0,1:T(8,128)S(1)}, u32[]{:S(2)}, u32[]{:S(2)}) %all-to-all-start.1) | async-done | bytes 262176 | tf_op jit(solution)/shard_map/all_to_all | solution.py:95
  98.8 1.1 fusion.23
  99.8 0.0 all-gather.3.cloned.1.call-update
  99.9 0.0 all-gather.5.cloned.1.call-start
  99.9 0.7 all-gather.5.cloned.1.call-update
  100.6 19.3 %all-gather.3.cloned.1.call-done = bf16[4096,128]{1,0:T(8,128)(2,1)} async-done(((bf16[512,128]{1,0:T(8,128)(2,1)}), bf16[4096,128]{1,0:T(8,128)(2,1)}) %all-gather.3.cloned.1.call-update) | async-done | bytes 1048592 | tf_op jit(solution)/shard_map/all_gather | solution.py:97
  120.0 160.3 %all-gather.5.cloned.1.call-done = bf16[4096,1024]{1,0:T(8,128)(2,1)} async-done(((bf16[64,1024]{1,0:T(8,128)(2,1)}), bf16[4096,1024]{1,0:T(8,128)(2,1)}) %all-gather.5.cloned.1.call-update) | async-done | bytes 8388624 | tf_op jit(solution)/shard_map/all_gather | solution.py:100
  280.3 5.7 %convolution_convert_fusion = bf16[128,1024]{1,0:T(8,128)(2,1)} fusion(bf16[4096,128]{1,0:T(8,128)(2,1)} %all-gather.3.cloned.1.call-done, bf16[4096,1024]{1,0:T(8,128)(2,1)} %all-gather.5.cloned.1.call-done), kind=kOutput, calls=%fused_computation.8 | convolution fusion | flops 1073872896 | bytes 9699328 | tf_op jit(solution)/shard_map/dot_general | solution.py:98
  (3 shorter events, 0.1 us)
Async XLA Ops:
  6.5 15.6 %copy-start.1 = (bf16[512,128]{1,0:T(8,128)(2,1)S(1)}, bf16[512,128]{1,0:T(8,128)(2,1)}, u32[]{:S(2)}) copy-start(bf16[512,128]{1,0:T(8,128)(2,1)} %param.7) | copy-start | bytes 393220
  6.5 15.6 %copy-start = (bf16[512,128]{1,0:T(8,128)(2,1)S(1)}, bf16[512,128]{1,0:T(8,128)(2,1)}, u32[]{:S(2)}) copy-start(bf16[512,128]{1,0:T(8,128)(2,1)} %param.8) | copy-start | bytes 393220
  10.3 11.8 %collective-permute-start = (bf16[3,512,2]{2,1,0:T(8,128)(2,1)S(1)}, bf16[3,512,2]{2,1,0:T(8,128)(2,1)S(1)}, u32[]{:S(2)}, u32[]{:S(2)}) collective-permute-start(bf16[3,512,2]{2,1,0:T(8,128)(2,1)S(1)} %copy.25), channel_id=1, source_target_pairs={{0,8},{8,16},{16,24},{24,32},{32,40},{40,48},{48,56},{56,64},{64,7... | collective-permute-start | bytes 18440 | tf_op jit(solution)/shard_map/ppermute | solution.py:13
  23.8 37.2 %all-to-all-start = ((bf16[64,8,128]{2,1,0:T(8,128)(2,1)}), bf16[64,8,128]{2,1,0:T(8,128)(2,1)S(1)}, u32[]{:S(2)}, u32[]{:S(2)}) async-start(bf16[64,8,128]{2,1,0:T(8,128)(2,1)} %fusion.47), calls=%async_computation | async-start | bytes 262144 | tf_op jit(solution)/shard_map/all_to_all | solution.py:93
  64.5 13.0 %copy-start.2 = (bf16[512,128]{1,0:T(8,128)(2,1)S(1)}, bf16[512,128]{1,0:T(8,128)(2,1)}, u32[]{:S(2)}) copy-start(bf16[512,128]{1,0:T(8,128)(2,1)} %param.6) | copy-start | bytes 393220
  72.8 26.0 %all-to-all-start.1 = ((f32[8,64,128]{2,0,1:T(8,128)}), f32[8,64,128]{2,0,1:T(8,128)S(1)}, u32[]{:S(2)}, u32[]{:S(2)}) async-start(f32[8,64,128]{2,0,1:T(8,128)} %copy.32), calls=%async_computation.1 | async-start | bytes 524288 | tf_op jit(solution)/shard_map/all_to_all | solution.py:95
  77.4 42.5 %all-gather.3.cloned.1.call-start = ((), (), s32[]{:S(2)}) async-start(), calls=%async_computation.2 | async-start | bytes 1179648 | tf_op jit(solution)/shard_map/all_gather | solution.py:97
  99.9 180.4 %all-gather.5.cloned.1.call-start = ((), (), s32[]{:S(2)}) async-start(), calls=%async_computation.3 | async-start | bytes 8519680 | tf_op jit(solution)/shard_map/all_gather | solution.py:100
Sparse Core Ops, SparseCore 0:
  100.0 19.9 all-gather.2
  122.9 157.3 all-gather.4
where the time goes:
time: 293 us
  waiting for transfers between devices  218 us (74%)
  starting transfers between devices  28.7 us (10%)
  matrix products  21.1 us (7%)
  between operations  13.7 us (5%)
  local copies, waits for them, and re-layouts  7.47 us (3%)
  other arithmetic  3.41 us (1%)
    all_gather x1, waiting for transfers between devices, shards(): lax.all_gather(out_weight, 'seq', axis=0, tiled=True)  160 us
    all_to_all x1, waiting for transfers between devices, shards(): lax.all_to_all(mixed_conv, 'seq', split_axis=1, concat_axis=0, tiled=True)  21.1 us
    all_to_all x1, starting transfers between devices, shards(): lax.all_to_all(product, 'seq', split_axis=0, concat_axis=1, tiled=True)  20.5 us
    all_gather x1, waiting for transfers between devices, shards(): full_rows = lax.all_gather(gated_out, 'tp', axis=0, tiled=True)  19.3 us
    all_to_all x1, waiting for transfers between devices, shards(): lax.all_to_all(product, 'seq', split_axis=0, concat_axis=1, tiled=True)  15.1 us
    dot_general x12, matrix products, right_apply(): return jnp.einsum('ckn,nm->ckm', signal, phase, precision=precise)  9.29 us
  transfers between devices with their start and end apart: 5, of which 5 were waited for; matrix products, arithmetic and copies ran while one was open for 3% of the time, Pallas kernels for 0%

commit v1 on v0

--- a/solution.py
+++ b/solution.py
@@ -94,7 +94,21 @@
     mixed_conv = long_convolve(spread.astype(jnp.float32), long_filters, inner_size)
     returned = lax.all_to_all(mixed_conv, "seq", split_axis=1, concat_axis=0, tiled=True)
     gated_out = (query_short * returned).astype(jnp.bfloat16)
-    full_rows = lax.all_gather(gated_out, "tp", axis=0, tiled=True)
+    num_devices = lax.psum(1, axis_name="tp")
+    table = [(d, (d + 1) % num_devices) for d in range(num_devices)]
+    shelf = [(d, (d - 1) % num_devices) for d in range(num_devices)]
+    heard, response = ([gated_out], [gated_out])
+    for _ in range(num_devices // 2):
+        block_next = lax.ppermute(heard[-1], axis_name="tp", perm=table)
+        heard.append(block_next)
+    hop_no = 0
+    while hop_no < (num_devices - 1) // 2:
+        top = lax.ppermute(response[-1], axis_name="tp", perm=shelf)
+        response.append(top)
+        hop_no += 1
+    local_now = jnp.concatenate([*heard[::-1], *response[1:]], axis=0)
+    built = lax.axis_index("tp")
+    full_rows = jnp.roll(local_now, (built - num_devices // 2) * gated_out.shape[0], axis=0)
     result = lax.dot_general(
         full_rows,
         lax.all_gather(out_weight, "seq", axis=0, tiled=True),

time: 293 us -> 186 us (0.63)
  waiting for transfers between devices: 218 us -> 107 us
  starting transfers between devices: 28.7 us -> 34.9 us
    all_gather x1, waiting for transfers between devices: 160 us -> 53.6 us  [shards(): lax.all_gather(out_weight, 'seq', axis=0, tiled=True)]
    all_gather x1 -> x0, waiting for transfers between devices: 19.3 us -> none  [shards(): full_rows = lax.all_gather(gated_out, 'tp', axis=0, tiled=True)]
    ppermute x0 -> x7, waiting for transfers between devices: none -> 11.9 us  [the longest x4 11.1 us: shards(): block_next = lax.ppermute(heard[-1], axis_name='tp', perm=table)]
    ppermute x0 -> x7, starting transfers between devices: none -> 6.18 us  [the longest x3 6.15 us: shards(): top = lax.ppermute(response[-1], axis_name='tp', perm=shelf)]
  transfers between devices with their start and end apart: 5 -> 11, of which waited for: 5 -> 10; matrix products, arithmetic and copies ran while one was open for 3% -> 13% of each run, Pallas kernels for 0% -> 0%
where the time goes in v1:
time: 186 us
  waiting for transfers between devices  107 us (58%)
  starting transfers between devices  34.9 us (19%)
  matrix products  20.8 us (11%)
  between operations  13.8 us (7%)
  local copies, waits for them, and re-layouts  6.88 us (4%)
  other arithmetic  2.75 us (1%)
    all_gather x1, waiting for transfers between devices, shards(): lax.all_gather(out_weight, 'seq', axis=0, tiled=True)  53.6 us
    all_to_all x1, waiting for transfers between devices, shards(): lax.all_to_all(mixed_conv, 'seq', split_axis=1, concat_axis=0, tiled=True)  21.9 us
    all_to_all x1, starting transfers between devices, shards(): lax.all_to_all(product, 'seq', split_axis=0, concat_axis=1, tiled=True)  20.5 us
    all_to_all x1, waiting for transfers between devices, shards(): lax.all_to_all(product, 'seq', split_axis=0, concat_axis=1, tiled=True)  16 us
    ppermute x4, waiting for transfers between devices, shards(): block_next = lax.ppermute(heard[-1], axis_name='tp', perm=table)  11.1 us
    dot_general x12, matrix products, right_apply(): return jnp.einsum('ckn,nm->ckm', signal, phase, precision=precise)  9.31 us
    ppermute x3, starting transfers between devices, shards(): top = lax.ppermute(response[-1], axis_name='tp', perm=shelf)  6.15 us
    dot_general x1, matrix products, shards(): lax.dot_general(full_rows, lax.all_gather(out_weight, 'seq', axis=0, tile...  5.37 us
  transfers between devices with their start and end apart: 11, of which 10 were waited for; matrix products, arithmetic and copies ran while one was open for 13% of the time, Pallas kernels for 0%

profile of v1, /device:TPU:2, one launch (start us, length us, event | category | flops | bytes accessed | tf_op | source)
XLA Modules:
  0.0 185.9 jit_solution(11645864898718294468)
XLA Ops:
  6.5 0.7 all-gather.2.cloned.1.call-update
  7.3 1.0 slice.94
  8.3 0.1 copy.35
  8.4 1.0 slice.95
  9.4 0.1 copy.36
  9.5 1.0 slice.96
  10.5 0.1 copy.37
  10.7 0.3 copy.25
  10.9 3.5 %collective-permute-start = (bf16[3,512,2]{2,1,0:T(8,128)(2,1)S(1)}, bf16[3,512,2]{2,1,0:T(8,128)(2,1)S(1)}, u32[]{:S(2)}, u32[]{:S(2)}) collective-permute-start(bf16[3,512,2]{2,1,0:T(8,128)(2,1)S(1)} %copy.25), channel_id=1, source_target_pairs={{0,8},{8,16},{16,24},{24,32},{32,40},{40,48},{48,56},{56,64},{64,7... | collective-permute-start | bytes 18440 | tf_op jit(solution)/shard_map/ppermute | solution.py:13
  14.5 1.1 reshape.82
  15.6 0.2 copy.29
  15.8 0.3 multiply_sine_fusion.1
  16.1 1.1 fusion.59
  17.2 1.1 fusion.62
  18.3 0.0 copy-start
  18.3 0.0 copy-start.1
  18.3 0.8 fusion.5
  19.1 0.8 convolution_add_fusion.1
  19.9 0.3 multiply_sine_fusion
  20.1 2.6 %collective-permute-done = bf16[3,512,2]{2,1,0:T(8,128)(2,1)S(1)} collective-permute-done((bf16[3,512,2]{2,1,0:T(8,128)(2,1)S(1)}, bf16[3,512,2]{2,1,0:T(8,128)(2,1)S(1)}, u32[]{:S(2)}, u32[]{:S(2)}) %collective-permute-start) | collective-permute-done | bytes 6176 | tf_op jit(solution)/shard_map/ppermute | solution.py:13
  22.8 0.0 copy-done
  22.8 0.2 maximum_convert_fusion.1
  23.1 1.4 fusion.48
  24.5 20.5 %all-to-all-start = ((bf16[64,8,128]{2,1,0:T(8,128)(2,1)}), bf16[64,8,128]{2,1,0:T(8,128)(2,1)S(1)}, u32[]{:S(2)}, u32[]{:S(2)}) async-start(bf16[64,8,128]{2,1,0:T(8,128)(2,1)} %fusion.48), calls=%async_computation | async-start | bytes 262144 | tf_op jit(solution)/shard_map/all_to_all | solution.py:93
  45.0 0.8 fusion.7
  45.8 0.8 convolution_subtract_fusion.1
  46.6 16.0 %all-to-all-done = bf16[64,8,128]{2,1,0:T(8,128)(2,1)S(1)} async-done(((bf16[64,8,128]{2,1,0:T(8,128)(2,1)}), bf16[64,8,128]{2,1,0:T(8,128)(2,1)S(1)}, u32[]{:S(2)}, u32[]{:S(2)}) %all-to-all-start) | async-done | bytes 131104 | tf_op jit(solution)/shard_map/all_to_all | solution.py:93
  62.6 0.1 reshape.81
  62.7 0.9 convolution_bitcast_fusion
  63.6 0.9 convolution_bitcast_fusion.1
  64.5 0.8 fusion.50
  65.3 0.8 fusion.49
  66.1 0.8 convolution_subtract_fusion.2
  66.9 0.9 multiply_add_fusion
  67.8 0.7 fusion.72
  68.6 0.7 fusion.68
  69.3 0.7 convolution_subtract_fusion
  70.0 0.7 convolution_add_fusion
  70.8 1.1 fusion.12
  71.9 0.0 copy-start.2
  71.9 1.1 fusion.1
  73.0 0.2 copy.31
  73.2 0.1 div.13
  73.3 1.1 copy.32
  74.4 4.7 %all-to-all-start.1 = ((f32[8,64,128]{2,0,1:T(8,128)}), f32[8,64,128]{2,0,1:T(8,128)S(1)}, u32[]{:S(2)}, u32[]{:S(2)}) async-start(f32[8,64,128]{2,0,1:T(8,128)} %copy.32), calls=%async_computation.1 | async-start | bytes 524288 | tf_op jit(solution)/shard_map/all_to_all | solution.py:95
  79.1 0.1 maximum_convert_fusion
  79.3 21.9 %all-to-all-done.1 = f32[8,64,128]{2,0,1:T(8,128)S(1)} async-done(((f32[8,64,128]{2,0,1:T(8,128)}), f32[8,64,128]{2,0,1:T(8,128)S(1)}, u32[]{:S(2)}, u32[]{:S(2)}) %all-to-all-start.1) | async-done | bytes 262176 | tf_op jit(solution)/shard_map/all_to_all | solution.py:95
  101.2 0.4 fusion.24
  101.6 0.0 collective-permute-start.1
  101.6 4.4 %collective-permute-done.1 = bf16[512,128]{1,0:T(8,128)(2,1)S(1)} collective-permute-done((bf16[512,128]{1,0:T(8,128)(2,1)S(1)}, bf16[512,128]{1,0:T(8,128)(2,1)S(1)}, u32[]{:S(2)}, u32[]{:S(2)}) %collective-permute-start.1) | collective-permute-done | bytes 131104 | tf_op jit(solution)/shard_map/ppermute | solution.py:102
  106.0 0.0 collective-permute-start.2
  106.0 1.7 collective-permute-start.5
  107.7 2.6 %collective-permute-done.2 = bf16[512,128]{1,0:T(8,128)(2,1)S(1)} collective-permute-done((bf16[512,128]{1,0:T(8,128)(2,1)S(1)}, bf16[512,128]{1,0:T(8,128)(2,1)S(1)}, u32[]{:S(2)}, u32[]{:S(2)}) %collective-permute-start.2) | collective-permute-done | bytes 131104 | tf_op jit(solution)/shard_map/ppermute | solution.py:102
  110.4 0.0 collective-permute-start.3
  110.4 0.0 collective-permute-done.5
  110.4 2.1 %collective-permute-start.6 = (bf16[512,128]{1,0:T(8,128)(2,1)S(1)}, bf16[512,128]{1,0:T(8,128)(2,1)S(1)}, u32[]{:S(2)}, u32[]{:S(2)}) collective-permute-start(bf16[512,128]{1,0:T(8,128)(2,1)S(1)} %collective-permute-done.5), channel_id=1, source_target_pairs={{0,7},{1,0},{2,1},{3,2},{4,3},{5,4},{6,5},{7,6},{8,15},{9,8},{10,9... | collective-permute-start | bytes 393224 | tf_op jit(solution)/shard_map/ppermute | solution.py:106
  112.5 2.2 %collective-permute-done.3 = bf16[512,128]{1,0:T(8,128)(2,1)S(1)} collective-permute-done((bf16[512,128]{1,0:T(8,128)(2,1)S(1)}, bf16[512,128]{1,0:T(8,128)(2,1)S(1)}, u32[]{:S(2)}, u32[]{:S(2)}) %collective-permute-start.3) | collective-permute-done | bytes 131104 | tf_op jit(solution)/shard_map/ppermute | solution.py:102
  114.8 0.0 collective-permute-start.4
  114.8 0.3 collective-permute-done.6
  115.0 2.3 %collective-permute-start.7 = (bf16[512,128]{1,0:T(8,128)(2,1)S(1)}, bf16[512,128]{1,0:T(8,128)(2,1)S(1)}, u32[]{:S(2)}, u32[]{:S(2)}) collective-permute-start(bf16[512,128]{1,0:T(8,128)(2,1)S(1)} %collective-permute-done.6), channel_id=1, source_target_pairs={{0,7},{1,0},{2,1},{3,2},{4,3},{5,4},{6,5},{7,6},{8,15},{9,8},{10,9... | collective-permute-start | bytes 393224 | tf_op jit(solution)/shard_map/ppermute | solution.py:106
  117.3 1.8 collective-permute-done.4
  119.3 0.5 collective-permute-done.7
  120.1 53.6 %all-gather.2.cloned.1.call-done = bf16[4096,1024]{1,0:T(8,128)(2,1)} async-done(((bf16[64,1024]{1,0:T(8,128)(2,1)}), bf16[4096,1024]{1,0:T(8,128)(2,1)}) %all-gather.2.cloned.1.call-update) | async-done | bytes 8388624 | tf_op jit(solution)/shard_map/all_gather | solution.py:114
  173.7 5.4 %convolution_convert_fusion = bf16[128,1024]{1,0:T(8,128)(2,1)} fusion(bf16[4096,1024]{1,0:T(8,128)(2,1)} %all-gather.2.cloned.1.call-done, bf16[8192,128]{1,0:T(8,128)(2,1)S(1)} %constant_dynamic-update-slice_fusion, s32[]{:T(128)S(6)} %select_n.117), kind=kOutput, calls=%fused_computation.8 | convolution fusion | flops 1073872896 | bytes 9699332 | tf_op jit(solution)/shard_map/dot_general | solution.py:112
  (25 shorter events, 0.4 us)
Async XLA Ops:
  6.5 9.5 %copy-start.3 = (f32[3,3,512]{2,1,0:T(4,128)S(1)}, f32[3,3,512]{2,1,0:T(4,128)}, u32[]{:S(2)}) copy-start(f32[3,3,512]{2,1,0:T(4,128)} %param.9) | copy-start | bytes 55300
  6.5 167.1 %all-gather.2.cloned.1.call-start = ((), (), s32[]{:S(2)}) async-start(), calls=%async_computation.2 | async-start | bytes 8519680 | tf_op jit(solution)/shard_map/all_gather | solution.py:114
  10.9 11.8 %collective-permute-start = (bf16[3,512,2]{2,1,0:T(8,128)(2,1)S(1)}, bf16[3,512,2]{2,1,0:T(8,128)(2,1)S(1)}, u32[]{:S(2)}, u32[]{:S(2)}) collective-permute-start(bf16[3,512,2]{2,1,0:T(8,128)(2,1)S(1)} %copy.25), channel_id=1, source_target_pairs={{0,8},{8,16},{16,24},{24,32},{32,40},{40,48},{48,56},{56,64},{64,7... | collective-permute-start | bytes 18440 | tf_op jit(solution)/shard_map/ppermute | solution.py:13
  18.3 4.5 %copy-start = (bf16[512,128]{1,0:T(8,128)(2,1)S(1)}, bf16[512,128]{1,0:T(8,128)(2,1)}, u32[]{:S(2)}) copy-start(bf16[512,128]{1,0:T(8,128)(2,1)} %param.8) | copy-start | bytes 393220
  18.3 4.5 %copy-start.1 = (bf16[512,128]{1,0:T(8,128)(2,1)S(1)}, bf16[512,128]{1,0:T(8,128)(2,1)}, u32[]{:S(2)}) copy-start(bf16[512,128]{1,0:T(8,128)(2,1)} %param.7) | copy-start | bytes 393220
  24.5 38.1 %all-to-all-start = ((bf16[64,8,128]{2,1,0:T(8,128)(2,1)}), bf16[64,8,128]{2,1,0:T(8,128)(2,1)S(1)}, u32[]{:S(2)}, u32[]{:S(2)}) async-start(bf16[64,8,128]{2,1,0:T(8,128)(2,1)} %fusion.48), calls=%async_computation | async-start | bytes 262144 | tf_op jit(solution)/shard_map/all_to_all | solution.py:93
  71.9 7.2 %copy-start.2 = (bf16[512,128]{1,0:T(8,128)(2,1)S(1)}, bf16[512,128]{1,0:T(8,128)(2,1)}, u32[]{:S(2)}) copy-start(bf16[512,128]{1,0:T(8,128)(2,1)} %param.6) | copy-start | bytes 393220
  74.4 26.7 %all-to-all-start.1 = ((f32[8,64,128]{2,0,1:T(8,128)}), f32[8,64,128]{2,0,1:T(8,128)S(1)}, u32[]{:S(2)}, u32[]{:S(2)}) async-start(f32[8,64,128]{2,0,1:T(8,128)} %copy.32), calls=%async_computation.1 | async-start | bytes 524288 | tf_op jit(solution)/shard_map/all_to_all | solution.py:95
  101.6 4.4 %collective-permute-start.1 = (bf16[512,128]{1,0:T(8,128)(2,1)S(1)}, bf16[512,128]{1,0:T(8,128)(2,1)S(1)}, u32[]{:S(2)}, u32[]{:S(2)}) collective-permute-start(bf16[512,128]{1,0:T(8,128)(2,1)S(1)} %fusion.24), channel_id=1, source_target_pairs={{0,1},{1,2},{2,3},{3,4},{4,5},{5,6},{6,7},{7,0},{8,9},{9,10},{10,1... | collective-permute-start | bytes 393224 | tf_op jit(solution)/shard_map/ppermute | solution.py:102
  106.0 4.4 %collective-permute-start.2 = (bf16[512,128]{1,0:T(8,128)(2,1)S(1)}, bf16[512,128]{1,0:T(8,128)(2,1)S(1)}, u32[]{:S(2)}, u32[]{:S(2)}) collective-permute-start(bf16[512,128]{1,0:T(8,128)(2,1)S(1)} %collective-permute-done.1), channel_id=1, source_target_pairs={{0,1},{1,2},{2,3},{3,4},{4,5},{5,6},{6,7},{7,0},{8,9},{9,10},{10,1... | collective-permute-start | bytes 393224 | tf_op jit(solution)/shard_map/ppermute | solution.py:102
  106.0 4.4 %collective-permute-start.5 = (bf16[512,128]{1,0:T(8,128)(2,1)S(1)}, bf16[512,128]{1,0:T(8,128)(2,1)S(1)}, u32[]{:S(2)}, u32[]{:S(2)}) collective-permute-start(bf16[512,128]{1,0:T(8,128)(2,1)S(1)} %fusion.24), channel_id=1, source_target_pairs={{0,7},{1,0},{2,1},{3,2},{4,3},{5,4},{6,5},{7,6},{8,15},{9,8},{10,9... | collective-permute-start | bytes 393224 | tf_op jit(solution)/shard_map/ppermute | solution.py:106
  110.4 4.4 %collective-permute-start.3 = (bf16[512,128]{1,0:T(8,128)(2,1)S(1)}, bf16[512,128]{1,0:T(8,128)(2,1)S(1)}, u32[]{:S(2)}, u32[]{:S(2)}) collective-permute-start(bf16[512,128]{1,0:T(8,128)(2,1)S(1)} %collective-permute-done.2), channel_id=1, source_target_pairs={{0,1},{1,2},{2,3},{3,4},{4,5},{5,6},{6,7},{7,0},{8,9},{9,10},{10,1... | collective-permute-start | bytes 393224 | tf_op jit(solution)/shard_map/ppermute | solution.py:102
  110.4 4.7 %collective-permute-start.6 = (bf16[512,128]{1,0:T(8,128)(2,1)S(1)}, bf16[512,128]{1,0:T(8,128)(2,1)S(1)}, u32[]{:S(2)}, u32[]{:S(2)}) collective-permute-start(bf16[512,128]{1,0:T(8,128)(2,1)S(1)} %collective-permute-done.5), channel_id=1, source_target_pairs={{0,7},{1,0},{2,1},{3,2},{4,3},{5,4},{6,5},{7,6},{8,15},{9,8},{10,9... | collective-permute-start | bytes 393224 | tf_op jit(solution)/shard_map/ppermute | solution.py:106
  114.8 4.4 %collective-permute-start.4 = (bf16[512,128]{1,0:T(8,128)(2,1)S(1)}, bf16[512,128]{1,0:T(8,128)(2,1)S(1)}, u32[]{:S(2)}, u32[]{:S(2)}) collective-permute-start(bf16[512,128]{1,0:T(8,128)(2,1)S(1)} %collective-permute-done.3), channel_id=1, source_target_pairs={{0,1},{1,2},{2,3},{3,4},{4,5},{5,6},{6,7},{7,0},{8,9},{9,10},{10,1... | collective-permute-start | bytes 393224 | tf_op jit(solution)/shard_map/ppermute | solution.py:102
  115.0 4.8 %collective-permute-start.7 = (bf16[512,128]{1,0:T(8,128)(2,1)S(1)}, bf16[512,128]{1,0:T(8,128)(2,1)S(1)}, u32[]{:S(2)}, u32[]{:S(2)}) collective-permute-start(bf16[512,128]{1,0:T(8,128)(2,1)S(1)} %collective-permute-done.6), channel_id=1, source_target_pairs={{0,7},{1,0},{2,1},{3,2},{4,3},{5,4},{6,5},{7,6},{8,15},{9,8},{10,9... | collective-permute-start | bytes 393224 | tf_op jit(solution)/shard_map/ppermute | solution.py:106
Sparse Core Ops, SparseCore 0:
  10.3 163.3 all-gather.1
